TPU v7x, 32 devices: a whole 2x2x4 slice. The times are simulated.
32 devices in a mesh: lon: 8 (over z, y), lat: 4 (over x, core).
Axes of the slice: x: 2, y: 2, z: 4, core: 2. Of those that a mesh axis runs over, the one named last changes fastest.
Arguments:
- crosswise_speed_units: float32 [8, 64, 2048], P(None, 'lat', 'lon'), may hold values from -6 to 6
- poleward_speed_units: float32 [8, 64, 2048], P(None, 'lat', 'lon'), may hold values from -6 to 6
- thermal_anomaly: float32 [8, 64, 2048], P(None, 'lat', 'lon'), may hold values from -6 to 6
- saltiness_anomaly: float32 [8, 64, 2048], P(None, 'lat', 'lon'), may hold values from -6 to 6
- freeboard_elevation: float32 [64, 2048], P('lat', 'lon'), may hold values from -6 to 6
- barotropic_zonal_flow: float32 [64, 2048], P('lat', 'lon'), may hold values from -6 to 6
- barotropic_meridional_flow: float32 [64, 2048], P('lat', 'lon'), may hold values from -6 to 6
- submerged_layer_tally: int32 [64, 2048], P('lat', 'lon'), may hold values from 0 to 8
- seam_partner_index: int32 [2048], P('lon'), may hold values from 0 to 2047, as said below
Outputs:
- zonal_speed_final: float32 [8, 64, 2048], P(None, 'lat', 'lon')
- poleward_speed_final: float32 [8, 64, 2048], P(None, 'lat', 'lon')
- thermal_final: float32 [8, 64, 2048], P(None, 'lat', 'lon')
- saltiness_final: float32 [8, 64, 2048], P(None, 'lat', 'lon')
- freeboard_final: float32 [64, 2048], P('lat', 'lon')
- barotropic_zonal_final: float32 [64, 2048], P('lat', 'lon')
- barotropic_meridional_final: float32 [64, 2048], P('lat', 'lon')
Inputs may be any that keep to these rules, and one draw needn't show every extreme that they name: seam_partner_index[seam_partner_index[c]] = c, and seam_partner_index[(c + 1) mod 2048] = (seam_partner_index[c] - 1) mod 2048 for every column c.
All inputs are finite; a program needn't handle non-finite values.
Results may differ from a plain program's by a relative error of at most 0.0003.
Values sent between devices are 32-bit elements; how exact they have to be, the bound alone decides.
No kernel may reach another device: no remote copies, remote signals or barrier semaphores. Data moves between devices by JAX's collectives and lax.ppermute only.
A program may use at most 128 MiB of HBM per device.

v0:
```python
import jax
import jax.numpy as jnp
from jax import lax
from jax.sharding import PartitionSpec as P

SUBSTEPS = 12
COURANT = 0.15
PRESSURE_GAIN = 0.1
CORIOLIS = 0.3
WAVE_MASS = 1.2
WAVE_MOMENTUM = 1.2
EPSILON = 1e-06


def extended_2(cells, sides, width, closed):
    for axis, dim in sides:
        count = lax.axis_size(axis)
        ends = count if closed else count - 1
        head = lax.slice_in_dim(cells, 0, width, axis=dim)
        tail = lax.slice_in_dim(cells, cells.shape[dim] - width, cells.shape[dim], axis=dim)
        cells = jnp.concatenate(
            [
                lax.ppermute(tail, axis, [(i, (i + 1) % count) for i in range(ends)]),
                cells,
                lax.ppermute(head, axis, [((i + 1) % count, i) for i in range(ends)]),
            ],
            axis=dim,
        )
    return cells


def weno_face(far_up, near_up, centre, near_down, far_down):
    poly_zero = (2.0 * far_up - 7.0 * near_up + 11.0 * centre) / 6.0
    poly_one = (-near_up + 5.0 * centre + 2.0 * near_down) / 6.0
    poly_two = (2.0 * centre + 5.0 * near_down - far_down) / 6.0
    smooth_zero = (
        13.0 / 12.0 * (far_up - 2.0 * near_up + centre) ** 2
        + 0.25 * (far_up - 4.0 * near_up + 3.0 * centre) ** 2
    )
    smooth_one = (
        13.0 / 12.0 * (near_up - 2.0 * centre + near_down) ** 2 + 0.25 * (near_up - near_down) ** 2
    )
    smooth_two = (
        13.0 / 12.0 * (centre - 2.0 * near_down + far_down) ** 2
        + 0.25 * (3.0 * centre - 4.0 * near_down + far_down) ** 2
    )
    weight_zero = 0.1 / (EPSILON + smooth_zero) ** 2
    weight_one = 0.6 / (EPSILON + smooth_one) ** 2
    weight_two = 0.3 / (EPSILON + smooth_two) ** 2
    return (weight_zero * poly_zero + weight_one * poly_one + weight_two * poly_two) / (
        weight_zero + weight_one + weight_two
    )


def face_fluxes(prognostic_bundle, velocity, wet_mask, along, length):

    def window(values, offset):
        return lax.slice_in_dim(values, offset, offset + length + 1, axis=along)

    face_speed = (
        0.5
        * (window(velocity, 2) + window(velocity, 3))
        * window(wet_mask, 2)
        * window(wet_mask, 3)
    )
    upwind = weno_face(
        window(prognostic_bundle, 0),
        window(prognostic_bundle, 1),
        window(prognostic_bundle, 2),
        window(prognostic_bundle, 3),
        window(prognostic_bundle, 4),
    )
    downwind = weno_face(
        window(prognostic_bundle, 5),
        window(prognostic_bundle, 4),
        window(prognostic_bundle, 3),
        window(prognostic_bundle, 2),
        window(prognostic_bundle, 1),
    )
    fluxes = COURANT * face_speed * jnp.where(face_speed >= 0.0, upwind, downwind)
    return (fluxes, face_speed)


def partner_fold(tops, parity, lead_offset, column_count, first_partner, northern, total_columns):
    facing = jnp.remainder(
        first_partner - lead_offset - lax.iota(jnp.int32, column_count), total_columns
    )
    picked = jnp.take(jnp.flip(tops, axis=1), facing, axis=2)
    return jnp.where(northern, parity * picked, 0.0)


def extend_deep(stacked_fields, parity, first_partner, northern, total_columns):
    channels, tile_rows, tile_cols = stacked_fields.shape
    east_west = extended_2(stacked_fields, (("lon", 2),), 3, True)
    north_south = extended_2(stacked_fields, (("lat", 1),), 3, False)
    tops = lax.all_gather(stacked_fields[:, tile_rows - 3 :, :], "lon", axis=2, tiled=True)
    ghosts = partner_fold(tops, parity, 0, tile_cols, first_partner, northern, total_columns)
    north_south = jnp.concatenate(
        [north_south[:, : tile_rows + 3], north_south[:, tile_rows + 3 :] + ghosts], axis=1
    )
    return (east_west, north_south)


def extend_wave(stacked_fields, margin, parity, first_partner, northern, total_columns):
    channels, tile_rows, tile_cols = stacked_fields.shape
    east_west = extended_2(stacked_fields, (("lon", 2),), margin, True)
    whole = extended_2(east_west, (("lat", 1),), margin, False)
    tops = lax.all_gather(stacked_fields[:, tile_rows - margin :, :], "lon", axis=2, tiled=True)
    ghosts = partner_fold(
        tops, parity, -margin, tile_cols + 2 * margin, first_partner, northern, total_columns
    )
    return jnp.concatenate(
        [whole[:, : tile_rows + margin], whole[:, tile_rows + margin :] + ghosts], axis=1
    )


def on_device(
    crosswise_speed_units,
    poleward_speed_units,
    thermal_anomaly,
    saltiness_anomaly,
    freeboard_elevation,
    barotropic_zonal_flow,
    barotropic_meridional_flow,
    submerged_layer_tally,
    seam_partner_index,
):
    levels, tile_rows, tile_cols = crosswise_speed_units.shape
    lat_size = lax.axis_size("lat")
    lon_size = lax.axis_size("lon")
    lat_index = lax.axis_index("lat")
    total_rows = tile_rows * lat_size
    total_columns = tile_cols * lon_size
    northern = lat_index == lat_size - 1
    first_partner = seam_partner_index[0]
    block_steps = 6
    margin = 2 * block_steps
    layer_total_real = submerged_layer_tally.astype(jnp.float32)
    stacked_fields = jnp.concatenate(
        [
            crosswise_speed_units,
            poleward_speed_units,
            thermal_anomaly,
            saltiness_anomaly,
            layer_total_real[None],
        ],
        axis=0,
    )
    parity = jnp.concatenate(
        [
            jnp.full((2 * levels, 1, 1), -1.0, jnp.float32),
            jnp.ones((2 * levels + 1, 1, 1), jnp.float32),
        ],
        axis=0,
    )
    east_west, north_south = extend_deep(
        stacked_fields, parity, first_partner, northern, total_columns
    )
    level_index = lax.broadcasted_iota(jnp.float32, (levels, 1, 1), 0)
    submerged_indicator = (level_index < layer_total_real[None]).astype(jnp.float32)
    wet_east = (level_index < east_west[4 * levels][None]).astype(jnp.float32)
    wet_north = (level_index < north_south[4 * levels][None]).astype(jnp.float32)
    fields_east = east_west[: 4 * levels].reshape(4, levels, tile_rows, tile_cols + 6)
    fields_north = north_south[: 4 * levels].reshape(4, levels, tile_rows + 6, tile_cols)
    flux_east, speed_east = face_fluxes(fields_east, fields_east[0:1], wet_east[None], 3, tile_cols)
    flux_north, speed_north = face_fluxes(
        fields_north, fields_north[1:2], wet_north[None], 2, tile_rows
    )
    prognostic_rate = -(flux_east[:, :, :, 1:] - flux_east[:, :, :, :-1]) - (
        flux_north[:, :, 1:, :] - flux_north[:, :, :-1, :]
    )
    spread = (
        speed_east[0, :, :, 1:]
        - speed_east[0, :, :, :-1]
        + (speed_north[0, :, 1:, :] - speed_north[0, :, :-1, :])
    )
    upward = -jnp.flip(jnp.cumsum(jnp.flip(spread, 0), axis=0), 0)
    prognostic_bundle = jnp.stack(
        [crosswise_speed_units, poleward_speed_units, thermal_anomaly, saltiness_anomaly], axis=0
    )
    interior = (
        COURANT * upward[None, 1:] * 0.5 * (prognostic_bundle[:, :-1] + prognostic_bundle[:, 1:])
    )
    boundary = jnp.zeros((4, 1, tile_rows, tile_cols), jnp.float32)
    vertical_flux = jnp.concatenate([boundary, interior, boundary], axis=1)
    prognostic_rate = prognostic_rate - (vertical_flux[:, :-1] - vertical_flux[:, 1:])
    density_east = 0.8 * fields_east[3] - 0.2 * fields_east[2]
    pressure_east = jnp.cumsum(density_east, axis=0) - 0.5 * density_east
    grad_east = 0.5 * (
        pressure_east[:, :, 4 : tile_cols + 4] - pressure_east[:, :, 2 : tile_cols + 2]
    )
    density_north = 0.8 * fields_north[3] - 0.2 * fields_north[2]
    pressure_north = jnp.cumsum(density_north, axis=0) - 0.5 * density_north
    grad_north = 0.5 * (
        pressure_north[:, 4 : tile_rows + 4, :] - pressure_north[:, 2 : tile_rows + 2, :]
    )
    own_rows = (lat_index * tile_rows + lax.iota(jnp.int32, tile_rows)).astype(jnp.float32)[:, None]
    coriolis = CORIOLIS * (2.0 * (own_rows + 0.5) / total_rows - 1.0)
    force_zonal = prognostic_rate[0] + coriolis * poleward_speed_units - PRESSURE_GAIN * grad_east
    force_merid = prognostic_rate[1] - coriolis * crosswise_speed_units - PRESSURE_GAIN * grad_north
    column = jnp.maximum(submerged_layer_tally, 1).astype(jnp.float32)
    mean_zonal = jnp.sum(submerged_indicator * force_zonal, axis=0) / column
    mean_merid = jnp.sum(submerged_indicator * force_merid, axis=0) / column
    static_parity = jnp.array([1.0, -1.0, -1.0], jnp.float32)[:, None, None]
    statics = extend_wave(
        jnp.stack([layer_total_real, mean_zonal, mean_merid], axis=0),
        margin,
        static_parity,
        first_partner,
        northern,
        total_columns,
    )
    thickness = statics[0] / levels
    wet_column = (statics[0] > 0.0).astype(jnp.float32)
    global_rows = lat_index * tile_rows - margin + lax.iota(jnp.int32, tile_rows + 2 * margin)
    mirrored = jnp.minimum(global_rows, 2 * total_rows - 1 - global_rows).astype(jnp.float32)[
        :, None
    ]
    coriolis_wide = CORIOLIS * (2.0 * (mirrored + 0.5) / total_rows - 1.0)

    def trim(values, keep):
        return values[
            margin - keep : margin + tile_rows + keep, margin - keep : margin + tile_cols + keep
        ]

    wave_parity = jnp.array([1.0, -1.0, -1.0], jnp.float32)[:, None, None]
    sea_level, zonal_flow, merid_flow = (
        freeboard_elevation,
        barotropic_zonal_flow,
        barotropic_meridional_flow,
    )
    for block in range(SUBSTEPS // block_steps):
        extended = extend_wave(
            jnp.stack([sea_level, zonal_flow, merid_flow], axis=0),
            margin,
            wave_parity,
            first_partner,
            northern,
            total_columns,
        )
        sea_level, zonal_flow, merid_flow = (extended[0], extended[1], extended[2])
        for inner_step in range(block_steps):
            outer = margin - 2 * inner_step
            keep = outer - 2
            thick = trim(thickness, outer)
            mass_east = thick * zonal_flow
            mass_north = thick * merid_flow
            spread_wave = 0.5 * (mass_east[1:-1, 2:] - mass_east[1:-1, :-2]) + 0.5 * (
                mass_north[2:, 1:-1] - mass_north[:-2, 1:-1]
            )
            next_level = trim(wet_column, outer - 1) * (
                sea_level[1:-1, 1:-1] - WAVE_MASS * spread_wave
            )
            rotation = coriolis_wide[margin - keep : margin + tile_rows + keep]
            wet_keep = trim(wet_column, keep)
            inner_zonal = zonal_flow[2:-2, 2:-2]
            inner_merid = merid_flow[2:-2, 2:-2]
            zonal_flow = wet_keep * (
                inner_zonal
                - WAVE_MOMENTUM * 0.5 * (next_level[1:-1, 2:] - next_level[1:-1, :-2])
                + (rotation * inner_merid + trim(statics[1], keep)) / SUBSTEPS
            )
            merid_flow = wet_keep * (
                inner_merid
                - WAVE_MOMENTUM * 0.5 * (next_level[2:, 1:-1] - next_level[:-2, 1:-1])
                + (-rotation * inner_zonal + trim(statics[2], keep)) / SUBSTEPS
            )
            sea_level = next_level[1:-1, 1:-1]
    zonal_speed_final = submerged_indicator * (
        crosswise_speed_units + force_zonal - mean_zonal + (zonal_flow - barotropic_zonal_flow)
    )
    poleward_speed_final = submerged_indicator * (
        poleward_speed_units + force_merid - mean_merid + (merid_flow - barotropic_meridional_flow)
    )
    thermal_final = submerged_indicator * (thermal_anomaly + prognostic_rate[2])
    saltiness_final = submerged_indicator * (saltiness_anomaly + prognostic_rate[3])
    return (
        zonal_speed_final,
        poleward_speed_final,
        thermal_final,
        saltiness_final,
        sea_level,
        zonal_flow,
        merid_flow,
    )


def solution(mesh):
    placed = (
        P(None, "lat", "lon"),
        P(None, "lat", "lon"),
        P(None, "lat", "lon"),
        P(None, "lat", "lon"),
        P("lat", "lon"),
        P("lat", "lon"),
        P("lat", "lon"),
        P("lat", "lon"),
        P("lon"),
    )
    return jax.shard_map(
        on_device,
        mesh=mesh,
        in_specs=placed,
        out_specs=(
            P(None, "lat", "lon"),
            P(None, "lat", "lon"),
            P(None, "lat", "lon"),
            P(None, "lat", "lon"),
            P("lat", "lon"),
            P("lat", "lon"),
            P("lat", "lon"),
        ),
        check_vma=False,
    )
```

profile of v0, /device:TPU:6, one launch (start us, length us, event | category | flops | bytes accessed | tf_op | source)
XLA Modules:
  0.0 298.3 jit_solution(17658706679827525291)
XLA Ops:
  8.2 3.0 %collective-permute-start.2 = (f32[33,3,256]{2,0,1:T(8,128)}, f32[33,3,256]{2,0,1:T(8,128)}, u32[]{:S(2)}, u32[]{:S(2)}) collective-permute-start(f32[33,3,256]{2,0,1:T(8,128)} %get-tuple-element.95), channel_id=1, source_target_pairs={{0,1},{1,2},{2,3},{4,5},{5,6},{6,7},{8,9},{9,10},{10,11},{12,13},{... | collective-permute-start | bytes 304136 | tf_op jit(solution)/shard_map/ppermute | solution.py:23
  13.3 4.6 %collective-permute-start.9 = (f32[3,16,12]{2,1,0:T(8,128)}, f32[3,16,12]{2,1,0:T(8,128)S(1)}, u32[]{:S(2)}, u32[]{:S(2)}) collective-permute-start(f32[3,16,12]{2,1,0:T(8,128)} %get-tuple-element.153), channel_id=1, source_target_pairs={{4,0},{8,4},{12,8},{16,12},{20,16},{24,20},{28,24},{0,28},{5,1},{9... | collective-permute-start | bytes 6920 | tf_op jit(solution)/shard_map/ppermute | solution.py:25
  17.9 33.4 %all_gather.12 = f32[33,3,2048]{2,0,1:T(8,128)S(1)} all-gather(f32[33,3,256]{2,0,1:T(8,128)} %get-tuple-element.95), channel_id=1, replica_groups=mesh['lon'=8,'lat'=4] {'lon'}, dimensions={2}, use_global_device_ids=true | all-gather | bytes 912384 | tf_op jit(solution)/shard_map/all_gather | solution.py:96
  60.5 31.6 %all_gather.14 = f32[3,12,2048]{2,1,0:T(8,128)S(1)} all-gather(f32[3,12,256]{2,1,0:T(8,128)} %slice.1172), channel_id=1, replica_groups=mesh['lon'=8,'lat'=4] {'lon'}, dimensions={2}, use_global_device_ids=true | all-gather | bytes 331776 | tf_op jit(solution)/shard_map/all_gather | solution.py:108
  93.3 3.1 %copy.196 = f32[33,3,2048]{0,1,2:T(4,128)} copy(f32[33,3,2048]{2,0,1:T(8,128)S(1)} %all_gather.12) | data formatting | bytes 1622016 | tf_op jit(solution)/shard_map/all_gather | solution.py:96
  96.4 11.6 %rev.21 = f32[33,3,2048]{0,1,2:T(4,128)} reverse(f32[33,3,2048]{0,1,2:T(4,128)} %copy.196), dimensions={1} | reverse | bytes 1622016 | tf_op jit(solution)/shard_map/jit(_flip)/rev | solution.py:88
  108.1 3.2 %gather_fusion = f32[256,33,3]{1,2,0:T(4,128)S(1)} fusion(f32[33,3,2048]{0,1,2:T(4,128)} %rev.21, s32[1024]{0:T(1024)S(1)} %pad_clamp_fusion.1), kind=kCustom, calls=%fused_computation.3 | custom fusion | bytes 203776 | tf_op jit(solution)/shard_map/jit(_take)/gather | solution.py:88
  112.1 3.2 %copy.214 = f32[3,12,2048]{1,0,2:T(4,128)} copy(f32[3,12,2048]{2,1,0:T(8,128)S(1)} %all_gather.14) | data formatting | bytes 589824 | tf_op jit(solution)/shard_map/all_gather | solution.py:108
  115.3 12.0 %rev.25 = f32[3,12,2048]{1,0,2:T(4,128)} reverse(f32[3,12,2048]{1,0,2:T(4,128)} %copy.214), dimensions={1} | reverse | bytes 589824 | tf_op jit(solution)/shard_map/jit(_flip)/rev | solution.py:88
  127.2 4.1 %gather_fusion.2 = f32[280,3,12]{2,1,0:T(4,128)} fusion(f32[3,12,2048]{1,0,2:T(4,128)} %rev.25, s32[1024]{0:T(1024)S(1)} %pad_clamp_fusion), kind=kCustom, calls=%fused_computation.1.clone | custom fusion | bytes 81760 | tf_op jit(solution)/shard_map/jit(_take)/gather | solution.py:88
  134.8 3.2 %collective-permute-start.10 = (f32[3,12,280]{2,1,0:T(8,128)}, f32[3,12,280]{2,1,0:T(8,128)}, u32[]{:S(2)}, u32[]{:S(2)}) collective-permute-start(f32[3,12,280]{2,1,0:T(8,128)} %get-tuple-element.146), channel_id=1, source_target_pairs={{0,1},{1,2},{2,3},{4,5},{5,6},{6,7},{8,9},{9,10},{10,11},{12,13},{... | collective-permute-start | bytes 120968 | tf_op jit(solution)/shard_map/ppermute | solution.py:23
  138.4 2.7 fusion.254
  143.5 5.4 %select_multiply_fusion = f32[4,8,16,257]{3,1,2,0:T(8,128)S(1)} fusion(f32[4,8,16,257]{3,2,1,0:T(8,128)} %get-tuple-element.88, f32[4,8,16,257]{3,2,1,0:T(8,128)S(1)} %get-tuple-element.84, f32[4,8,16,257]{3,2,1,0:T(8,128)} %get-tuple-element.85, f32[4,8,16,257]{3,2,1,0:T(8,128)} %get-tuple-element.86, f32[4,8,16,257]{3,2,1,0:T(8,128)} %get-tuple-element.87, ...), kind=kLoop, calls=%fused_computation.6 | loop fusion | flops 16579584 | bytes 3848832 | tf_op jit(solution)/shard_map/mul | solution.py:80
  158.8 3.7 %select_multiply_fusion.1 = f32[4,8,17,256]{3,1,2,0:T(8,128)S(1)} fusion(f32[4,8,17,256]{3,1,0,2:T(8,128)} %get-tuple-element.94, f32[4,8,17,256]{3,1,0,2:T(8,128)S(1)} %get-tuple-element.90, f32[4,8,17,256]{3,1,0,2:T(8,128)} %get-tuple-element.91, f32[4,8,17,256]{3,1,0,2:T(8,128)} %get-tuple-element.92, f32[4,8,17,256]{3,1,0,2:T(8,128)} %get-tuple-element.93, ...), kind=kLoop, calls=%fused_computation.40 | loop fusion | flops 17547264 | bytes 4073472 | tf_op jit(solution)/shard_map/mul | solution.py:80
  163.4 3.5 %collective-permute-start.5 = (f32[3,16,12]{2,1,0:T(8,128)S(1)}, f32[3,16,12]{2,1,0:T(8,128)S(1)}, u32[]{:S(2)}, u32[]{:S(2)}) collective-permute-start(f32[3,16,12]{2,1,0:T(8,128)S(1)} %get-tuple-element.155), channel_id=1, source_target_pairs={{4,0},{8,4},{12,8},{16,12},{20,16},{24,20},{28,24},{0,28},{5,1},{9... | collective-permute-start | bytes 6920 | tf_op jit(solution)/shard_map/ppermute | solution.py:25
  166.9 33.2 %all_gather.13 = f32[3,12,2048]{2,1,0:T(8,128)S(1)} all-gather(f32[3,12,256]{2,1,0:T(8,128)S(1)} %slice.1154), channel_id=1, replica_groups=mesh['lon'=8,'lat'=4] {'lon'}, dimensions={2}, use_global_device_ids=true | all-gather | bytes 331776 | tf_op jit(solution)/shard_map/all_gather | solution.py:108
  200.1 3.1 %copy.212 = f32[3,12,2048]{1,0,2:T(4,128)} copy(f32[3,12,2048]{2,1,0:T(8,128)S(1)} %all_gather.13) | data formatting | bytes 589824 | tf_op jit(solution)/shard_map/all_gather | solution.py:108
  203.3 12.0 %rev.24 = f32[3,12,2048]{1,0,2:T(4,128)} reverse(f32[3,12,2048]{1,0,2:T(4,128)} %copy.212), dimensions={1} | reverse | bytes 589824 | tf_op jit(solution)/shard_map/jit(_flip)/rev | solution.py:88
  215.3 3.3 %gather_fusion.1 = f32[280,3,12]{2,1,0:T(4,128)S(1)} fusion(f32[3,12,2048]{1,0,2:T(4,128)} %rev.24, s32[1024]{0:T(1024)S(1)} %copy-done.29), kind=kCustom, calls=%fused_computation.clone | custom fusion | bytes 81760 | tf_op jit(solution)/shard_map/jit(_take)/gather | solution.py:88
  232.2 2.9 collective-permute-start.12
  235.1 32.8 %all_gather.15 = f32[3,12,2048]{2,1,0:T(8,128)S(1)} all-gather(f32[3,12,256]{2,1,0:T(8,128)S(1)} %slice.1266), channel_id=1, replica_groups=mesh['lon'=8,'lat'=4] {'lon'}, dimensions={2}, use_global_device_ids=true | all-gather | bytes 331776 | tf_op jit(solution)/shard_map/all_gather | solution.py:108
  267.9 3.1 %copy.216 = f32[3,12,2048]{1,0,2:T(4,128)} copy(f32[3,12,2048]{2,1,0:T(8,128)S(1)} %all_gather.15) | data formatting | bytes 589824 | tf_op jit(solution)/shard_map/all_gather | solution.py:108
  271.0 12.0 %rev.26 = f32[3,12,2048]{1,0,2:T(4,128)} reverse(f32[3,12,2048]{1,0,2:T(4,128)} %copy.216), dimensions={1} | reverse | bytes 589824 | tf_op jit(solution)/shard_map/jit(_flip)/rev | solution.py:88
  283.0 3.2 %gather_fusion.3 = f32[280,3,12]{2,1,0:T(4,128)S(1)} fusion(f32[3,12,2048]{1,0,2:T(4,128)} %rev.26, s32[1024]{0:T(1024)S(1)} %copy-done.29), kind=kCustom, calls=%fused_computation.2.clone | custom fusion | bytes 81760 | tf_op jit(solution)/shard_map/jit(_take)/gather | solution.py:88
  (245 shorter events, 62.0 us)
Async XLA Ops:
  0.6 58.8 %copy-start.4 = (f32[8,16,256]{2,1,0:T(8,128)S(1)}, f32[8,16,256]{2,1,0:T(8,128)}, u32[]{:S(2)}) copy-start(f32[8,16,256]{2,1,0:T(8,128)} %param.13) | copy-start | bytes 393220
  0.6 58.7 %copy-start.6 = (f32[8,16,256]{2,1,0:T(8,128)S(1)}, f32[8,16,256]{2,1,0:T(8,128)}, u32[]{:S(2)}) copy-start(f32[8,16,256]{2,1,0:T(8,128)} %param.14) | copy-start | bytes 393220
  0.7 58.7 %copy-start.8 = (f32[8,16,256]{2,1,0:T(8,128)S(1)}, f32[8,16,256]{2,1,0:T(8,128)}, u32[]{:S(2)}) copy-start(f32[8,16,256]{2,1,0:T(8,128)} %param.15) | copy-start | bytes 393220
  0.7 58.7 %copy-start.10 = (f32[8,16,256]{2,1,0:T(8,128)S(1)}, f32[8,16,256]{2,1,0:T(8,128)}, u32[]{:S(2)}) copy-start(f32[8,16,256]{2,1,0:T(8,128)} %param.16) | copy-start | bytes 393220
  0.7 52.9 %copy-start.22 = (s32[16,256]{1,0:T(8,128)S(1)}, s32[16,256]{1,0:T(8,128)}, u32[]{:S(2)}) copy-start(s32[16,256]{1,0:T(8,128)} %param.20) | copy-start | bytes 49156
  0.7 50.6 %copy-start.47 = (s32[256]{0:T(256)S(1)}, s32[256]{0:T(256)}, u32[]{:S(2)}) copy-start(s32[256]{0:T(256)} %param.21) | copy-start | bytes 3076
  6.2 142.7 %collective-permute-start.3 = (f32[33,3,256]{2,0,1:T(8,128)}, f32[33,3,256]{2,0,1:T(8,128)}, u32[]{:S(2)}, u32[]{:S(2)}) collective-permute-start(f32[33,3,256]{2,0,1:T(8,128)} %get-tuple-element.96), channel_id=1, source_target_pairs={{1,0},{2,1},{3,2},{5,4},{6,5},{7,6},{9,8},{10,9},{11,10},{13,12},{... | collective-permute-start | bytes 304136 | tf_op jit(solution)/shard_map/ppermute | solution.py:25
  8.2 141.9 %collective-permute-start.2 = (f32[33,3,256]{2,0,1:T(8,128)}, f32[33,3,256]{2,0,1:T(8,128)}, u32[]{:S(2)}, u32[]{:S(2)}) collective-permute-start(f32[33,3,256]{2,0,1:T(8,128)} %get-tuple-element.95), channel_id=1, source_target_pairs={{0,1},{1,2},{2,3},{4,5},{5,6},{6,7},{8,9},{9,10},{10,11},{12,13},{... | collective-permute-start | bytes 304136 | tf_op jit(solution)/shard_map/ppermute | solution.py:23
  11.3 123.4 %collective-permute-start.1 = (f32[33,16,3]{2,1,0:T(8,128)S(1)}, f32[33,16,3]{2,1,0:T(8,128)S(1)}, u32[]{:S(2)}, u32[]{:S(2)}) collective-permute-start(f32[33,16,3]{2,1,0:T(8,128)S(1)} %get-tuple-element.104), channel_id=1, source_target_pairs={{4,0},{8,4},{12,8},{16,12},{20,16},{24,20},{28,24},{0,28},{5,1},{9... | collective-permute-start | bytes 19016 | tf_op jit(solution)/shard_map/ppermute | solution.py:25
  13.3 118.0 %collective-permute-start.9 = (f32[3,16,12]{2,1,0:T(8,128)}, f32[3,16,12]{2,1,0:T(8,128)S(1)}, u32[]{:S(2)}, u32[]{:S(2)}) collective-permute-start(f32[3,16,12]{2,1,0:T(8,128)} %get-tuple-element.153), channel_id=1, source_target_pairs={{4,0},{8,4},{12,8},{16,12},{20,16},{24,20},{28,24},{0,28},{5,1},{9... | collective-permute-start | bytes 6920 | tf_op jit(solution)/shard_map/ppermute | solution.py:25
  17.9 113.4 %collective-permute-start.8 = (f32[3,16,12]{2,1,0:T(8,128)}, f32[3,16,12]{2,1,0:T(8,128)}, u32[]{:S(2)}, u32[]{:S(2)}) collective-permute-start(f32[3,16,12]{2,1,0:T(8,128)} %get-tuple-element.152), channel_id=1, source_target_pairs={{0,4},{4,8},{8,12},{12,16},{16,20},{20,24},{24,28},{28,0},{1,5},{5... | collective-permute-start | bytes 6920 | tf_op jit(solution)/shard_map/ppermute | solution.py:23
  92.7 34.5 %copy-start.28 = (s32[1024]{0:T(1024)}, s32[1024]{0:T(1024)S(1)}, u32[]{:S(2)}) copy-start(s32[1024]{0:T(1024)S(1)} %pad_clamp_fusion) | copy-start | bytes 12292
  131.3 6.7 %collective-permute-start = (f32[33,16,3]{2,1,0:T(8,128)S(1)}, f32[33,16,3]{2,1,0:T(8,128)S(1)}, u32[]{:S(2)}, u32[]{:S(2)}) collective-permute-start(f32[33,16,3]{2,1,0:T(8,128)S(1)} %get-tuple-element.103), channel_id=1, source_target_pairs={{0,4},{4,8},{8,12},{12,16},{16,20},{20,24},{24,28},{28,0},{1,5},{5... | collective-permute-start | bytes 19016 | tf_op jit(solution)/shard_map/ppermute | solution.py:23
  132.8 87.1 %collective-permute-start.11 = (f32[3,12,280]{2,1,0:T(8,128)}, f32[3,12,280]{2,1,0:T(8,128)}, u32[]{:S(2)}, u32[]{:S(2)}) collective-permute-start(f32[3,12,280]{2,1,0:T(8,128)} %get-tuple-element.147), channel_id=1, source_target_pairs={{1,0},{2,1},{3,2},{5,4},{6,5},{7,6},{9,8},{10,9},{11,10},{13,12},{... | collective-permute-start | bytes 120968 | tf_op jit(solution)/shard_map/ppermute | solution.py:25
  134.8 86.1 %collective-permute-start.10 = (f32[3,12,280]{2,1,0:T(8,128)}, f32[3,12,280]{2,1,0:T(8,128)}, u32[]{:S(2)}, u32[]{:S(2)}) collective-permute-start(f32[3,12,280]{2,1,0:T(8,128)} %get-tuple-element.146), channel_id=1, source_target_pairs={{0,1},{1,2},{2,3},{4,5},{5,6},{6,7},{8,9},{9,10},{10,11},{12,13},{... | collective-permute-start | bytes 120968 | tf_op jit(solution)/shard_map/ppermute | solution.py:23
  163.4 58.6 %collective-permute-start.5 = (f32[3,16,12]{2,1,0:T(8,128)S(1)}, f32[3,16,12]{2,1,0:T(8,128)S(1)}, u32[]{:S(2)}, u32[]{:S(2)}) collective-permute-start(f32[3,16,12]{2,1,0:T(8,128)S(1)} %get-tuple-element.155), channel_id=1, source_target_pairs={{4,0},{8,4},{12,8},{16,12},{20,16},{24,20},{28,24},{0,28},{5,1},{9... | collective-permute-start | bytes 6920 | tf_op jit(solution)/shard_map/ppermute | solution.py:25
  166.9 55.1 %collective-permute-start.4 = (f32[3,16,12]{2,1,0:T(8,128)S(1)}, f32[3,16,12]{2,1,0:T(8,128)S(1)}, u32[]{:S(2)}, u32[]{:S(2)}) collective-permute-start(f32[3,16,12]{2,1,0:T(8,128)S(1)} %get-tuple-element.154), channel_id=1, source_target_pairs={{0,4},{4,8},{8,12},{12,16},{16,20},{20,24},{24,28},{28,0},{1,5},{5... | collective-permute-start | bytes 6920 | tf_op jit(solution)/shard_map/ppermute | solution.py:23
  203.3 18.7 %copy-start.19 = (f32[1,16,256]{2,1,0:T(8,128)S(1)}, f32[1,16,256]{2,1,0:T(8,128)}, u32[]{:S(2)}) copy-start(f32[1,16,256]{2,1,0:T(8,128)} %get-tuple-element.160) | copy-start | bytes 49156
  222.1 6.3 %collective-permute-start.7 = (f32[3,12,280]{2,1,0:T(8,128)S(1)}, f32[3,12,280]{2,1,0:T(8,128)S(1)}, u32[]{:S(2)}, u32[]{:S(2)}) collective-permute-start(f32[3,12,280]{2,1,0:T(8,128)S(1)} %get-tuple-element.149), channel_id=1, source_target_pairs={{1,0},{2,1},{3,2},{5,4},{6,5},{7,6},{9,8},{10,9},{11,10},{13,12},{... | collective-permute-start | bytes 120968 | tf_op jit(solution)/shard_map/ppermute | solution.py:25
  224.1 5.7 %collective-permute-start.6 = (f32[3,12,280]{2,1,0:T(8,128)S(1)}, f32[3,12,280]{2,1,0:T(8,128)S(1)}, u32[]{:S(2)}, u32[]{:S(2)}) collective-permute-start(f32[3,12,280]{2,1,0:T(8,128)S(1)} %get-tuple-element.148), channel_id=1, source_target_pairs={{0,1},{1,2},{2,3},{4,5},{5,6},{6,7},{8,9},{9,10},{10,11},{12,13},{... | collective-permute-start | bytes 120968 | tf_op jit(solution)/shard_map/ppermute | solution.py:23
  232.1 54.1 %collective-permute-start.13 = (f32[3,16,12]{2,1,0:T(8,128)S(1)}, f32[3,16,12]{2,1,0:T(8,128)S(1)}, u32[]{:S(2)}, u32[]{:S(2)}) collective-permute-start(f32[3,16,12]{2,1,0:T(8,128)S(1)} %get-tuple-element.151), channel_id=1, source_target_pairs={{4,0},{8,4},{12,8},{16,12},{20,16},{24,20},{28,24},{0,28},{5,1},{9... | collective-permute-start | bytes 6920 | tf_op jit(solution)/shard_map/ppermute | solution.py:25
  232.2 54.0 %collective-permute-start.12 = (f32[3,16,12]{2,1,0:T(8,128)S(1)}, f32[3,16,12]{2,1,0:T(8,128)S(1)}, u32[]{:S(2)}, u32[]{:S(2)}) collective-permute-start(f32[3,16,12]{2,1,0:T(8,128)S(1)} %get-tuple-element.150), channel_id=1, source_target_pairs={{0,4},{4,8},{8,12},{12,16},{16,20},{20,24},{24,28},{28,0},{1,5},{5... | collective-permute-start | bytes 6920 | tf_op jit(solution)/shard_map/ppermute | solution.py:23
  286.3 5.6 %collective-permute-start.15 = (f32[3,12,280]{2,1,0:T(8,128)S(1)}, f32[3,12,280]{2,1,0:T(8,128)S(1)}, u32[]{:S(2)}, u32[]{:S(2)}) collective-permute-start(f32[3,12,280]{2,1,0:T(8,128)S(1)} %get-tuple-element.145), channel_id=1, source_target_pairs={{1,0},{2,1},{3,2},{5,4},{6,5},{7,6},{9,8},{10,9},{11,10},{13,12},{... | collective-permute-start | bytes 120968 | tf_op jit(solution)/shard_map/ppermute | solution.py:25
  288.3 5.7 %collective-permute-start.14 = (f32[3,12,280]{2,1,0:T(8,128)S(1)}, f32[3,12,280]{2,1,0:T(8,128)S(1)}, u32[]{:S(2)}, u32[]{:S(2)}) collective-permute-start(f32[3,12,280]{2,1,0:T(8,128)S(1)} %get-tuple-element.144), channel_id=1, source_target_pairs={{0,1},{1,2},{2,3},{4,5},{5,6},{6,7},{8,9},{9,10},{10,11},{12,13},{... | collective-permute-start | bytes 120968 | tf_op jit(solution)/shard_map/ppermute | solution.py:23
  (40 other events, 402.1 us)
where the time goes:
time: 301 us; the launch traced here: 298 us
  blocking collectives  131 us (44%)
  local copies, waits for them, and re-layouts  91.7 us (30%)
  other arithmetic  39.2 us (13%)
  starting transfers between devices  30.5 us (10%)
  waiting for transfers between devices  3.36 us (1%)
    all_gather x3, blocking collectives, extend_wave(): lax.all_gather(stacked_fields[:, tile_rows - margin:, :], 'lon', axis=2,...  97.6 us
    rev x4, local copies, waits for them, and re-layouts, partner_fold(): picked = jnp.take(jnp.flip(tops, axis=1), facing, axis=2)  47.5 us
    all_gather x1, blocking collectives, extend_deep(): lax.all_gather(stacked_fields[:, tile_rows - 3:, :], 'lon', axis=2, tiled...  33.4 us
    ppermute x8, starting transfers between devices, extended_2(): lax.ppermute(head, axis, [((i + 1) % count, i) for i in range(ends)])  16.4 us
    gather x5, local copies, waits for them, and re-layouts, partner_fold(): picked = jnp.take(jnp.flip(tops, axis=1), facing, axis=2)  14.6 us
    ppermute x8, starting transfers between devices, extended_2(): lax.ppermute(tail, axis, [(i, (i + 1) % count) for i in range(ends)])  14.1 us
    mul x4, other arithmetic, face_fluxes(): COURANT * face_speed * jnp.where(face_speed >= 0.0, upwind, downwind)  10.5 us
    all_gather x3, local copies, waits for them, and re-layouts, extend_wave(): lax.all_gather(stacked_fields[:, tile_rows - margin:, :], 'lon', axis=2,...  9.4 us
  transfers between devices with their start and end apart: 16, of which 2 were waited for; matrix products, arithmetic and copies ran while one was open for 40% of the time, Pallas kernels for 0%

commit v1 on v0

--- a/solution.py
+++ b/solution.py
@@ -105,7 +105,9 @@
     channels, tile_rows, tile_cols = stacked_fields.shape
     east_west = extended_2(stacked_fields, (("lon", 2),), margin, True)
     whole = extended_2(east_west, (("lat", 1),), margin, False)
-    tops = lax.all_gather(stacked_fields[:, tile_rows - margin :, :], "lon", axis=2, tiled=True)
+    tops = jnp.concatenate(
+        lax.all_gather(stacked_fields[:, tile_rows - margin :, :], "lon"), axis=2
+    )
     ghosts = partner_fold(
         tops, parity, -margin, tile_cols + 2 * margin, first_partner, northern, total_columns
     )

time: 301 us -> 300 us (level)
    all_gather x3 -> x0, local copies, waits for them, and re-layouts: 9.4 us -> none  [extend_wave(): lax.all_gather(stacked_fields[:, tile_rows - margin:, :], 'lon', axis=2,...]
    reshape x0 -> x3, local copies, waits for them, and re-layouts: none -> 9.39 us  [extend_wave(): jnp.concatenate(lax.all_gather(stacked_fields[:, tile_rows - margin:, :],...]
where the time goes in v1:
time: 300 us; the launch traced here: 298 us
  blocking collectives  131 us (44%)
  local copies, waits for them, and re-layouts  91.7 us (31%)
  other arithmetic  39.2 us (13%)
  starting transfers between devices  30.5 us (10%)
  waiting for transfers between devices  3.36 us (1%)
    all_gather x3, blocking collectives, extend_wave(): lax.all_gather(stacked_fields[:, tile_rows - margin:, :], 'lon')  97.6 us
    rev x4, local copies, waits for them, and re-layouts, partner_fold(): picked = jnp.take(jnp.flip(tops, axis=1), facing, axis=2)  47.5 us
    all_gather x1, blocking collectives, extend_deep(): lax.all_gather(stacked_fields[:, tile_rows - 3:, :], 'lon', axis=2, tiled...  33.4 us
    ppermute x8, starting transfers between devices, extended_2(): lax.ppermute(head, axis, [((i + 1) % count, i) for i in range(ends)])  16.4 us
    gather x5, local copies, waits for them, and re-layouts, partner_fold(): picked = jnp.take(jnp.flip(tops, axis=1), facing, axis=2)  14.6 us
    ppermute x8, starting transfers between devices, extended_2(): lax.ppermute(tail, axis, [(i, (i + 1) % count) for i in range(ends)])  14.1 us
    mul x4, other arithmetic, face_fluxes(): COURANT * face_speed * jnp.where(face_speed >= 0.0, upwind, downwind)  10.5 us
    reshape x3, local copies, waits for them, and re-layouts, extend_wave(): jnp.concatenate(lax.all_gather(stacked_fields[:, tile_rows - margin:, :],...  9.39 us
  transfers between devices with their start and end apart: 16, of which 2 were waited for; matrix products, arithmetic and copies ran while one was open for 40% of the time, Pallas kernels for 0%

profile of v1, /device:TPU:6, one launch (start us, length us, event | category | flops | bytes accessed | tf_op | source)
XLA Modules:
  0.0 298.3 jit_solution(12981026127346943061)
XLA Ops:
  8.2 3.0 %collective-permute-start.2 = (f32[33,3,256]{2,0,1:T(8,128)}, f32[33,3,256]{2,0,1:T(8,128)}, u32[]{:S(2)}, u32[]{:S(2)}) collective-permute-start(f32[33,3,256]{2,0,1:T(8,128)} %get-tuple-element.95), channel_id=1, source_target_pairs={{0,1},{1,2},{2,3},{4,5},{5,6},{6,7},{8,9},{9,10},{10,11},{12,13},{... | collective-permute-start | bytes 304136 | tf_op jit(solution)/shard_map/ppermute | solution.py:23
  13.3 4.6 %collective-permute-start.9 = (f32[3,16,12]{2,1,0:T(8,128)}, f32[3,16,12]{2,1,0:T(8,128)S(1)}, u32[]{:S(2)}, u32[]{:S(2)}) collective-permute-start(f32[3,16,12]{2,1,0:T(8,128)} %get-tuple-element.153), channel_id=1, source_target_pairs={{4,0},{8,4},{12,8},{16,12},{20,16},{24,20},{28,24},{0,28},{5,1},{9... | collective-permute-start | bytes 6920 | tf_op jit(solution)/shard_map/ppermute | solution.py:25
  17.9 33.4 %all_gather.21 = f32[33,3,2048]{2,0,1:T(8,128)S(1)} all-gather(f32[33,3,256]{2,0,1:T(8,128)} %get-tuple-element.95), channel_id=1, replica_groups=mesh['lon'=8,'lat'=4] {'lon'}, dimensions={2}, use_global_device_ids=true | all-gather | bytes 912384 | tf_op jit(solution)/shard_map/all_gather | solution.py:96
  60.5 31.6 %all-gather.1 = f32[24,12,256]{2,1,0:T(8,128)S(1)} all-gather(f32[3,12,256]{2,1,0:T(8,128)} %slice.1172), channel_id=3, replica_groups=mesh['lon'=8,'lat'=4] {'lon'}, dimensions={0}, use_global_device_ids=true | all-gather | bytes 331776 | tf_op jit(solution)/shard_map/all_gather | solution.py:109
  93.3 3.1 %copy.216 = f32[33,3,2048]{0,1,2:T(4,128)} copy(f32[33,3,2048]{2,0,1:T(8,128)S(1)} %all_gather.21) | data formatting | bytes 1622016 | tf_op jit(solution)/shard_map/all_gather | solution.py:96
  96.4 11.6 %rev.21 = f32[33,3,2048]{0,1,2:T(4,128)} reverse(f32[33,3,2048]{0,1,2:T(4,128)} %copy.216), dimensions={1} | reverse | bytes 1622016 | tf_op jit(solution)/shard_map/jit(_flip)/rev | solution.py:88
  108.1 3.2 %gather_fusion = f32[256,33,3]{1,2,0:T(4,128)S(1)} fusion(f32[33,3,2048]{0,1,2:T(4,128)} %rev.21, s32[1024]{0:T(1024)S(1)} %pad_clamp_fusion.1), kind=kCustom, calls=%fused_computation.3 | custom fusion | bytes 203776 | tf_op jit(solution)/shard_map/jit(_take)/gather | solution.py:88
  112.1 3.2 %copy.251 = f32[3,12,8,256]{1,0,3,2:T(4,128)} copy(f32[3,12,8,256]{3,1,0,2:T(8,128)S(1)} %bitcast.165) | data formatting | bytes 589824 | tf_op jit(solution)/shard_map/reshape | solution.py:108
  115.3 12.0 %rev.25 = f32[3,12,2048]{1,0,2:T(4,128)} reverse(f32[3,12,2048]{1,0,2:T(4,128)} %bitcast.159), dimensions={1} | reverse | bytes 589824 | tf_op jit(solution)/shard_map/jit(_flip)/rev | solution.py:88
  127.2 4.1 %gather_fusion.2 = f32[280,3,12]{2,1,0:T(4,128)} fusion(f32[3,12,2048]{1,0,2:T(4,128)} %rev.25, s32[1024]{0:T(1024)S(1)} %pad_clamp_fusion), kind=kCustom, calls=%fused_computation.1.clone | custom fusion | bytes 81760 | tf_op jit(solution)/shard_map/jit(_take)/gather | solution.py:88
  134.8 3.2 %collective-permute-start.10 = (f32[3,12,280]{2,1,0:T(8,128)}, f32[3,12,280]{2,1,0:T(8,128)}, u32[]{:S(2)}, u32[]{:S(2)}) collective-permute-start(f32[3,12,280]{2,1,0:T(8,128)} %get-tuple-element.146), channel_id=1, source_target_pairs={{0,1},{1,2},{2,3},{4,5},{5,6},{6,7},{8,9},{9,10},{10,11},{12,13},{... | collective-permute-start | bytes 120968 | tf_op jit(solution)/shard_map/ppermute | solution.py:23
  138.4 2.7 fusion.254
  143.5 5.4 %select_multiply_fusion = f32[4,8,16,257]{3,1,2,0:T(8,128)S(1)} fusion(f32[4,8,16,257]{3,2,1,0:T(8,128)} %get-tuple-element.88, f32[4,8,16,257]{3,2,1,0:T(8,128)S(1)} %get-tuple-element.84, f32[4,8,16,257]{3,2,1,0:T(8,128)} %get-tuple-element.85, f32[4,8,16,257]{3,2,1,0:T(8,128)} %get-tuple-element.86, f32[4,8,16,257]{3,2,1,0:T(8,128)} %get-tuple-element.87, ...), kind=kLoop, calls=%fused_computation.6 | loop fusion | flops 16579584 | bytes 3848832 | tf_op jit(solution)/shard_map/mul | solution.py:80
  158.8 3.7 %select_multiply_fusion.1 = f32[4,8,17,256]{3,1,2,0:T(8,128)S(1)} fusion(f32[4,8,17,256]{3,1,0,2:T(8,128)} %get-tuple-element.94, f32[4,8,17,256]{3,1,0,2:T(8,128)S(1)} %get-tuple-element.90, f32[4,8,17,256]{3,1,0,2:T(8,128)} %get-tuple-element.91, f32[4,8,17,256]{3,1,0,2:T(8,128)} %get-tuple-element.92, f32[4,8,17,256]{3,1,0,2:T(8,128)} %get-tuple-element.93, ...), kind=kLoop, calls=%fused_computation.40 | loop fusion | flops 17547264 | bytes 4073472 | tf_op jit(solution)/shard_map/mul | solution.py:80
  163.4 3.5 %collective-permute-start.5 = (f32[3,16,12]{2,1,0:T(8,128)S(1)}, f32[3,16,12]{2,1,0:T(8,128)S(1)}, u32[]{:S(2)}, u32[]{:S(2)}) collective-permute-start(f32[3,16,12]{2,1,0:T(8,128)S(1)} %get-tuple-element.155), channel_id=1, source_target_pairs={{4,0},{8,4},{12,8},{16,12},{20,16},{24,20},{28,24},{0,28},{5,1},{9... | collective-permute-start | bytes 6920 | tf_op jit(solution)/shard_map/ppermute | solution.py:25
  166.9 33.2 %all-gather = f32[24,12,256]{2,1,0:T(8,128)S(1)} all-gather(f32[3,12,256]{2,1,0:T(8,128)S(1)} %slice.1154), channel_id=2, replica_groups=mesh['lon'=8,'lat'=4] {'lon'}, dimensions={0}, use_global_device_ids=true | all-gather | bytes 331776 | tf_op jit(solution)/shard_map/all_gather | solution.py:109
  200.1 3.1 %copy.256 = f32[8,3,12,256]{2,1,3,0:T(4,128)} copy(f32[8,3,12,256]{3,2,1,0:T(8,128)S(1)} %bitcast.166) | data formatting | bytes 589824 | tf_op jit(solution)/shard_map/reshape | solution.py:108
  203.3 12.0 %rev.24 = f32[3,12,2048]{1,0,2:T(4,128)} reverse(f32[3,12,2048]{1,0,2:T(4,128)} %bitcast.160), dimensions={1} | reverse | bytes 589824 | tf_op jit(solution)/shard_map/jit(_flip)/rev | solution.py:88
  215.3 3.3 %gather_fusion.1 = f32[280,3,12]{2,1,0:T(4,128)S(1)} fusion(f32[3,12,2048]{1,0,2:T(4,128)} %rev.24, s32[1024]{0:T(1024)S(1)} %copy-done.29), kind=kCustom, calls=%fused_computation.clone | custom fusion | bytes 81760 | tf_op jit(solution)/shard_map/jit(_take)/gather | solution.py:88
  232.2 2.9 collective-permute-start.12
  235.1 32.8 %all-gather.2 = f32[24,12,256]{2,1,0:T(8,128)S(1)} all-gather(f32[3,12,256]{2,1,0:T(8,128)S(1)} %slice.1266), channel_id=4, replica_groups=mesh['lon'=8,'lat'=4] {'lon'}, dimensions={0}, use_global_device_ids=true | all-gather | bytes 331776 | tf_op jit(solution)/shard_map/all_gather | solution.py:109
  267.9 3.1 %copy.252 = f32[3,12,8,256]{1,0,3,2:T(4,128)} copy(f32[3,12,8,256]{3,1,0,2:T(8,128)S(1)} %bitcast.167) | data formatting | bytes 589824 | tf_op jit(solution)/shard_map/reshape | solution.py:108
  271.0 12.0 %rev.26 = f32[3,12,2048]{1,0,2:T(4,128)} reverse(f32[3,12,2048]{1,0,2:T(4,128)} %bitcast.161), dimensions={1} | reverse | bytes 589824 | tf_op jit(solution)/shard_map/jit(_flip)/rev | solution.py:88
  282.9 3.2 %gather_fusion.3 = f32[280,3,12]{2,1,0:T(4,128)S(1)} fusion(f32[3,12,2048]{1,0,2:T(4,128)} %rev.26, s32[1024]{0:T(1024)S(1)} %copy-done.29), kind=kCustom, calls=%fused_computation.2.clone | custom fusion | bytes 81760 | tf_op jit(solution)/shard_map/jit(_take)/gather | solution.py:88
  (245 shorter events, 62.0 us)
Async XLA Ops:
  0.6 58.8 %copy-start.4 = (f32[8,16,256]{2,1,0:T(8,128)S(1)}, f32[8,16,256]{2,1,0:T(8,128)}, u32[]{:S(2)}) copy-start(f32[8,16,256]{2,1,0:T(8,128)} %param.13) | copy-start | bytes 393220
  0.6 58.7 %copy-start.6 = (f32[8,16,256]{2,1,0:T(8,128)S(1)}, f32[8,16,256]{2,1,0:T(8,128)}, u32[]{:S(2)}) copy-start(f32[8,16,256]{2,1,0:T(8,128)} %param.14) | copy-start | bytes 393220
  0.7 58.7 %copy-start.8 = (f32[8,16,256]{2,1,0:T(8,128)S(1)}, f32[8,16,256]{2,1,0:T(8,128)}, u32[]{:S(2)}) copy-start(f32[8,16,256]{2,1,0:T(8,128)} %param.15) | copy-start | bytes 393220
  0.7 58.7 %copy-start.10 = (f32[8,16,256]{2,1,0:T(8,128)S(1)}, f32[8,16,256]{2,1,0:T(8,128)}, u32[]{:S(2)}) copy-start(f32[8,16,256]{2,1,0:T(8,128)} %param.16) | copy-start | bytes 393220
  0.7 52.9 %copy-start.22 = (s32[16,256]{1,0:T(8,128)S(1)}, s32[16,256]{1,0:T(8,128)}, u32[]{:S(2)}) copy-start(s32[16,256]{1,0:T(8,128)} %param.20) | copy-start | bytes 49156
  0.7 50.6 %copy-start.47 = (s32[256]{0:T(256)S(1)}, s32[256]{0:T(256)}, u32[]{:S(2)}) copy-start(s32[256]{0:T(256)} %param.21) | copy-start | bytes 3076
  6.2 142.7 %collective-permute-start.3 = (f32[33,3,256]{2,0,1:T(8,128)}, f32[33,3,256]{2,0,1:T(8,128)}, u32[]{:S(2)}, u32[]{:S(2)}) collective-permute-start(f32[33,3,256]{2,0,1:T(8,128)} %get-tuple-element.96), channel_id=1, source_target_pairs={{1,0},{2,1},{3,2},{5,4},{6,5},{7,6},{9,8},{10,9},{11,10},{13,12},{... | collective-permute-start | bytes 304136 | tf_op jit(solution)/shard_map/ppermute | solution.py:25
  8.2 141.9 %collective-permute-start.2 = (f32[33,3,256]{2,0,1:T(8,128)}, f32[33,3,256]{2,0,1:T(8,128)}, u32[]{:S(2)}, u32[]{:S(2)}) collective-permute-start(f32[33,3,256]{2,0,1:T(8,128)} %get-tuple-element.95), channel_id=1, source_target_pairs={{0,1},{1,2},{2,3},{4,5},{5,6},{6,7},{8,9},{9,10},{10,11},{12,13},{... | collective-permute-start | bytes 304136 | tf_op jit(solution)/shard_map/ppermute | solution.py:23
  11.3 123.4 %collective-permute-start.1 = (f32[33,16,3]{2,1,0:T(8,128)S(1)}, f32[33,16,3]{2,1,0:T(8,128)S(1)}, u32[]{:S(2)}, u32[]{:S(2)}) collective-permute-start(f32[33,16,3]{2,1,0:T(8,128)S(1)} %get-tuple-element.104), channel_id=1, source_target_pairs={{4,0},{8,4},{12,8},{16,12},{20,16},{24,20},{28,24},{0,28},{5,1},{9... | collective-permute-start | bytes 19016 | tf_op jit(solution)/shard_map/ppermute | solution.py:25
  13.3 118.0 %collective-permute-start.9 = (f32[3,16,12]{2,1,0:T(8,128)}, f32[3,16,12]{2,1,0:T(8,128)S(1)}, u32[]{:S(2)}, u32[]{:S(2)}) collective-permute-start(f32[3,16,12]{2,1,0:T(8,128)} %get-tuple-element.153), channel_id=1, source_target_pairs={{4,0},{8,4},{12,8},{16,12},{20,16},{24,20},{28,24},{0,28},{5,1},{9... | collective-permute-start | bytes 6920 | tf_op jit(solution)/shard_map/ppermute | solution.py:25
  17.9 113.4 %collective-permute-start.8 = (f32[3,16,12]{2,1,0:T(8,128)}, f32[3,16,12]{2,1,0:T(8,128)}, u32[]{:S(2)}, u32[]{:S(2)}) collective-permute-start(f32[3,16,12]{2,1,0:T(8,128)} %get-tuple-element.152), channel_id=1, source_target_pairs={{0,4},{4,8},{8,12},{12,16},{16,20},{20,24},{24,28},{28,0},{1,5},{5... | collective-permute-start | bytes 6920 | tf_op jit(solution)/shard_map/ppermute | solution.py:23
  92.7 34.5 %copy-start.28 = (s32[1024]{0:T(1024)}, s32[1024]{0:T(1024)S(1)}, u32[]{:S(2)}) copy-start(s32[1024]{0:T(1024)S(1)} %pad_clamp_fusion) | copy-start | bytes 12292
  131.3 6.7 %collective-permute-start = (f32[33,16,3]{2,1,0:T(8,128)S(1)}, f32[33,16,3]{2,1,0:T(8,128)S(1)}, u32[]{:S(2)}, u32[]{:S(2)}) collective-permute-start(f32[33,16,3]{2,1,0:T(8,128)S(1)} %get-tuple-element.103), channel_id=1, source_target_pairs={{0,4},{4,8},{8,12},{12,16},{16,20},{20,24},{24,28},{28,0},{1,5},{5... | collective-permute-start | bytes 19016 | tf_op jit(solution)/shard_map/ppermute | solution.py:23
  132.8 87.1 %collective-permute-start.11 = (f32[3,12,280]{2,1,0:T(8,128)}, f32[3,12,280]{2,1,0:T(8,128)}, u32[]{:S(2)}, u32[]{:S(2)}) collective-permute-start(f32[3,12,280]{2,1,0:T(8,128)} %get-tuple-element.147), channel_id=1, source_target_pairs={{1,0},{2,1},{3,2},{5,4},{6,5},{7,6},{9,8},{10,9},{11,10},{13,12},{... | collective-permute-start | bytes 120968 | tf_op jit(solution)/shard_map/ppermute | solution.py:25
  134.8 86.1 %collective-permute-start.10 = (f32[3,12,280]{2,1,0:T(8,128)}, f32[3,12,280]{2,1,0:T(8,128)}, u32[]{:S(2)}, u32[]{:S(2)}) collective-permute-start(f32[3,12,280]{2,1,0:T(8,128)} %get-tuple-element.146), channel_id=1, source_target_pairs={{0,1},{1,2},{2,3},{4,5},{5,6},{6,7},{8,9},{9,10},{10,11},{12,13},{... | collective-permute-start | bytes 120968 | tf_op jit(solution)/shard_map/ppermute | solution.py:23
  163.4 58.6 %collective-permute-start.5 = (f32[3,16,12]{2,1,0:T(8,128)S(1)}, f32[3,16,12]{2,1,0:T(8,128)S(1)}, u32[]{:S(2)}, u32[]{:S(2)}) collective-permute-start(f32[3,16,12]{2,1,0:T(8,128)S(1)} %get-tuple-element.155), channel_id=1, source_target_pairs={{4,0},{8,4},{12,8},{16,12},{20,16},{24,20},{28,24},{0,28},{5,1},{9... | collective-permute-start | bytes 6920 | tf_op jit(solution)/shard_map/ppermute | solution.py:25
  166.9 55.1 %collective-permute-start.4 = (f32[3,16,12]{2,1,0:T(8,128)S(1)}, f32[3,16,12]{2,1,0:T(8,128)S(1)}, u32[]{:S(2)}, u32[]{:S(2)}) collective-permute-start(f32[3,16,12]{2,1,0:T(8,128)S(1)} %get-tuple-element.154), channel_id=1, source_target_pairs={{0,4},{4,8},{8,12},{12,16},{16,20},{20,24},{24,28},{28,0},{1,5},{5... | collective-permute-start | bytes 6920 | tf_op jit(solution)/shard_map/ppermute | solution.py:23
  203.3 18.7 %copy-start.19 = (f32[1,16,256]{2,1,0:T(8,128)S(1)}, f32[1,16,256]{2,1,0:T(8,128)}, u32[]{:S(2)}) copy-start(f32[1,16,256]{2,1,0:T(8,128)} %get-tuple-element.160) | copy-start | bytes 49156
  222.1 6.3 %collective-permute-start.7 = (f32[3,12,280]{2,1,0:T(8,128)S(1)}, f32[3,12,280]{2,1,0:T(8,128)S(1)}, u32[]{:S(2)}, u32[]{:S(2)}) collective-permute-start(f32[3,12,280]{2,1,0:T(8,128)S(1)} %get-tuple-element.149), channel_id=1, source_target_pairs={{1,0},{2,1},{3,2},{5,4},{6,5},{7,6},{9,8},{10,9},{11,10},{13,12},{... | collective-permute-start | bytes 120968 | tf_op jit(solution)/shard_map/ppermute | solution.py:25
  224.1 5.7 %collective-permute-start.6 = (f32[3,12,280]{2,1,0:T(8,128)S(1)}, f32[3,12,280]{2,1,0:T(8,128)S(1)}, u32[]{:S(2)}, u32[]{:S(2)}) collective-permute-start(f32[3,12,280]{2,1,0:T(8,128)S(1)} %get-tuple-element.148), channel_id=1, source_target_pairs={{0,1},{1,2},{2,3},{4,5},{5,6},{6,7},{8,9},{9,10},{10,11},{12,13},{... | collective-permute-start | bytes 120968 | tf_op jit(solution)/shard_map/ppermute | solution.py:23
  232.1 54.1 %collective-permute-start.13 = (f32[3,16,12]{2,1,0:T(8,128)S(1)}, f32[3,16,12]{2,1,0:T(8,128)S(1)}, u32[]{:S(2)}, u32[]{:S(2)}) collective-permute-start(f32[3,16,12]{2,1,0:T(8,128)S(1)} %get-tuple-element.151), channel_id=1, source_target_pairs={{4,0},{8,4},{12,8},{16,12},{20,16},{24,20},{28,24},{0,28},{5,1},{9... | collective-permute-start | bytes 6920 | tf_op jit(solution)/shard_map/ppermute | solution.py:25
  232.2 54.0 %collective-permute-start.12 = (f32[3,16,12]{2,1,0:T(8,128)S(1)}, f32[3,16,12]{2,1,0:T(8,128)S(1)}, u32[]{:S(2)}, u32[]{:S(2)}) collective-permute-start(f32[3,16,12]{2,1,0:T(8,128)S(1)} %get-tuple-element.150), channel_id=1, source_target_pairs={{0,4},{4,8},{8,12},{12,16},{16,20},{20,24},{24,28},{28,0},{1,5},{5... | collective-permute-start | bytes 6920 | tf_op jit(solution)/shard_map/ppermute | solution.py:23
  286.3 5.6 %collective-permute-start.15 = (f32[3,12,280]{2,1,0:T(8,128)S(1)}, f32[3,12,280]{2,1,0:T(8,128)S(1)}, u32[]{:S(2)}, u32[]{:S(2)}) collective-permute-start(f32[3,12,280]{2,1,0:T(8,128)S(1)} %get-tuple-element.145), channel_id=1, source_target_pairs={{1,0},{2,1},{3,2},{5,4},{6,5},{7,6},{9,8},{10,9},{11,10},{13,12},{... | collective-permute-start | bytes 120968 | tf_op jit(solution)/shard_map/ppermute | solution.py:25
  288.3 5.7 %collective-permute-start.14 = (f32[3,12,280]{2,1,0:T(8,128)S(1)}, f32[3,12,280]{2,1,0:T(8,128)S(1)}, u32[]{:S(2)}, u32[]{:S(2)}) collective-permute-start(f32[3,12,280]{2,1,0:T(8,128)S(1)} %get-tuple-element.144), channel_id=1, source_target_pairs={{0,1},{1,2},{2,3},{4,5},{5,6},{6,7},{8,9},{9,10},{10,11},{12,13},{... | collective-permute-start | bytes 120968 | tf_op jit(solution)/shard_map/ppermute | solution.py:23
  (40 other events, 402.1 us)
